TPU v7x, 256 devices: a whole 4x4x8 slice. The times are simulated.
256 devices in a mesh: img: 32 (over y, z), ori: 8 (over x, core).
Axes of the slice: x: 4, y: 4, z: 8, core: 2. Of those that a mesh axis runs over, the one named last changes fastest.
Arguments:
- images: bfloat16 [1024, 2, 16256], P('img'), may hold values from -6 to 6
- shifts: int32 [1024], P('img'), may hold values from 0 to 35
- inv_temp: float32 [1024], P('img'), may hold values from 0.5 to 4
- candidates: int32 [32, 512], P('img'), may hold values from 0 to 1023
- volume: bfloat16 [64, 2, 16256], P(None, None, 'img'), may hold values from -6 to 6
- tilts: bfloat16 [1024, 64], P('ori'), may hold values from -1 to 1
- azimuth: float32 [1024], P('ori'), may hold values from -3.140625 to 3.140625
Outputs:
- posteriors: float32 [1024, 1024], P('img', 'ori')
- weighted_sums: float32 [16256, 2, 1024], P('img', None, 'ori')
- volume_grad: float32 [64, 2, 16256], P(None, None, 'img')
Inputs may be any that keep to these rules, and one draw needn't show every extreme that they name: `candidates`: A group's list may name an orientation more than once.
All inputs are finite; a program needn't handle non-finite values.
Results may differ from a plain program's by a relative error of at most 0.017.
Values may be sent and summed in bfloat16 or wider, within the bound.
No kernel may reach another device: no remote copies, remote signals or barrier semaphores. Data moves between devices by JAX's collectives and lax.ppermute only.
A program may use at most 128 MiB of HBM per device.

v0:
```python
import math
import jax
import jax.numpy as jnp
from jax import lax
from jax.sharding import Mesh
from jax.sharding import PartitionSpec as P

NSHIFT = 36
IMG = ("img_0", "img_1")
noise_var = 128.0
masked_fill = -1e30


def sent_to_all(x, axis):
    devices = lax.axis_size(axis)
    return lax.all_to_all(jnp.broadcast_to(x[None], (devices, *x.shape)), axis, 0, 0, tiled=True)


def of_everyone(x, axis):
    return sent_to_all(x, axis).max(axis=0)


def of_everyone_2(x, axis):
    everything = sent_to_all(x, axis)
    return jnp.sum(everything, axis=0)


def split_up(x, dim, devices):
    before, after = (x.shape[:dim], x.shape[dim + 1 :])
    return jnp.moveaxis(x.reshape(*before, devices, -1, *after), dim, 0)


def cut_rows(length, count):
    unit = 8 if length >= 8 * count else 1
    return [length // unit * k // count * unit for k in range(1, count)]


def own_block(tiles, axes, turns):
    inside = tiles.shape[1:]
    tiles = tiles.reshape(*(lax.axis_size(a) for a in axes), *inside)
    tiles = jnp.moveaxis(tiles, turns, range(len(axes))).reshape(-1, *inside)
    for k in turns:
        tiles = lax.psum_scatter(tiles, axes[k], scatter_dimension=0, tiled=True)
    return tiles[0]


def sum_at_once(x, axes, dim):
    tiles = split_up(x, dim, lax.axis_size(axes))
    widest = max(range(1, max(2, tiles.ndim - 1)), key=lambda d: tiles.shape[d])
    count, gathered = (len(axes), [])
    for first, share in enumerate(
        jnp.split(tiles, cut_rows(tiles.shape[widest], count), axis=widest)
    ):
        if share.size:
            turns = [(first + k) % count for k in range(count)]
            gathered.append(own_block(share, axes, turns))
    return jnp.concatenate(gathered, axis=widest - 1)


def over_copies(x, axis):
    everything = sent_to_all(x, axis)
    return jnp.sum(everything.astype(jnp.float32), axis=0)


def order_table(start, width):
    return ((start + jnp.arange(width, dtype=jnp.int32)) % 64 - 32).astype(jnp.float32)


def project_piece(piece, start, tilts, azimuth):
    width = piece.shape[2]
    degrees = piece.shape[0]
    mixed = jnp.dot(tilts, piece.reshape(degrees, 2 * width), preferred_element_type=jnp.float32)
    mixed = mixed.reshape(tilts.shape[0], 2, width)
    angles = azimuth[:, None] * order_table(start, width)[None, :]
    cosine = jnp.cos(angles)
    sine = jnp.sin(angles)
    real_part = mixed[:, 0] * cosine - mixed[:, 1] * sine
    imag_part = mixed[:, 0] * sine + mixed[:, 1] * cosine
    return jnp.stack([real_part, imag_part], axis=1).astype(jnp.bfloat16)


def rotate_images(images, shifts):
    width = images.shape[2]
    phase = shifts.astype(jnp.float32) * (2.0 * math.pi / NSHIFT)
    angles = phase[:, None] * order_table(0, width)[None, :]
    cosine = jnp.cos(angles)
    sine = jnp.sin(angles)
    first = images[:, 0].astype(jnp.float32)
    second = images[:, 1].astype(jnp.float32)
    real_part = first * cosine - second * sine
    imag_part = first * sine + second * cosine
    return jnp.stack([real_part, imag_part], axis=1).astype(jnp.bfloat16)


def shards(images, shifts, inv_temp, candidates, volume, tilts, azimuth):
    local_orients = tilts.shape[0]
    part_width = volume.shape[2]
    full_width = images.shape[2]
    image_count = images.shape[0]
    column_start = lax.axis_index(IMG) * part_width
    orient_ids = lax.axis_index("ori") * local_orients + jnp.arange(local_orients, dtype=jnp.int32)
    own_part = project_piece(volume, column_start, tilts, azimuth)
    slices = lax.all_gather(own_part, IMG, axis=2, tiled=True)
    rotated = rotate_images(images, shifts)
    flat_images = rotated.reshape(image_count, 2 * full_width)
    flat_slices = slices.reshape(local_orients, 2 * full_width)
    inner = lax.dot_general(
        flat_images, flat_slices, (((1,), (1,)), ((), ())), preferred_element_type=jnp.float32
    )
    energies = jnp.sum(jnp.square(slices.astype(jnp.float32)), axis=(1, 2))
    scores = inv_temp[:, None] * (inner - 0.5 * energies[None, :]) / noise_var
    allowed = jnp.any(candidates[0][:, None] == orient_ids[None, :], axis=0)
    allowed_rows = jnp.broadcast_to(allowed[None, :], scores.shape)
    held = jnp.where(allowed_rows, scores, masked_fill)
    local_peak = jnp.max(held, axis=1)
    peak = of_everyone(local_peak, "ori")
    local_total = jnp.sum(jnp.where(allowed_rows, jnp.exp(held - peak[:, None]), 0.0), axis=1)
    total = of_everyone_2(local_total, "ori")
    posteriors = jnp.where(allowed_rows, jnp.exp(held - peak[:, None]), 0.0) / total[:, None]
    post_bf = posteriors.astype(jnp.bfloat16)
    mass = of_everyone_2(jnp.sum(posteriors, axis=0), IMG)
    sums = sum_at_once(
        jnp.einsum("ick,io->kco", rotated, post_bf, preferred_element_type=jnp.float32).astype(
            jnp.bfloat16
        ),
        IMG,
        0,
    ).astype(jnp.float32)
    own_slices = lax.dynamic_slice_in_dim(slices, column_start, part_width, 2)
    own = jnp.transpose(own_slices.astype(jnp.float32), (2, 1, 0))
    resid = sums - mass[None, None, :] * own
    angles = order_table(column_start, part_width)[:, None] * azimuth[None, :]
    cosine = jnp.cos(angles)
    sine = jnp.sin(angles)
    back_real = resid[:, 0] * cosine + resid[:, 1] * sine
    back_imag = resid[:, 1] * cosine - resid[:, 0] * sine
    back = jnp.stack([back_real, back_imag], axis=1)
    partial_grad = (
        jnp.einsum("kco,ol->lck", back, tilts.astype(jnp.float32), precision=lax.Precision.HIGHEST)
        / noise_var
    )
    volume_grad = over_copies(partial_grad.astype(jnp.bfloat16), "ori").astype(jnp.float32)
    return (posteriors, sums, volume_grad)


def solution(mesh):
    finer = Mesh(mesh.devices.reshape(4, 8, mesh.shape["ori"]), ("img_0", "img_1", "ori"))
    return jax.shard_map(
        shards,
        mesh=finer,
        in_specs=(
            P(IMG, None, None),
            P(IMG),
            P(IMG),
            P(IMG, None),
            P(None, None, IMG),
            P("ori", None),
            P("ori"),
        ),
        out_specs=(P(IMG, "ori"), P(IMG, None, "ori"), P(None, None, IMG)),
        check_vma=False,
    )
```

profile of v0, /device:TPU:1, one launch (start us, length us, event | category | flops | bytes accessed | tf_op | source)
XLA Modules:
  0.0 394.1 jit_solution(1204516911856662296)
XLA Ops:
  7.3 1.2 reshape.337
  8.9 1.8 fusion.42
  10.8 0.9 copy.50
  11.9 3.0 fusion.66
  14.9 8.0 %fusion.8 = (bf16[32,1,16256]{2,0,1:T(8,128)(2,1)S(1)}, bf16[32,1,16256]{2,0,1:T(8,128)(2,1)S(1)}) fusion(f32[16256]{0:T(1024)S(1)} %fusion.48, f32[32]{0:T(128)S(1)} %convert_multiply_fusion, bf16[32,1,16256]{2,1,0:T(2,128)(2,1)S(1)} %get-tuple-element.23, bf16[32,1,16256]{2,1,0:T(2,128)(2,1)S(1)} %get-tuple-element.22), kind=kLoop, calls=%fused_computation.14 | loop fusion | flops 5722112 | bytes 4226688 | tf_op jit(solution)/shard_map/convert.2
  22.9 89.6 %all-gather.2.cloned.1.call-done = bf16[128,2,16256]{0,1,2:T(2,128)(2,1)} async-done(((bf16[128,2,508]{0,1,2:T(2,128)(2,1)}), bf16[128,2,16256]{0,1,2:T(2,128)(2,1)}) %all-gather.2.cloned.1.call-update) | async-done | bytes 8323088 | tf_op jit(solution)/shard_map/all_gather | solution.py:103
  112.5 18.5 %multiply_reduce_fusion = f32[128]{0:T(128)S(1)} fusion(bf16[128,2,16256]{0,1,2:T(2,128)(2,1)} %all-gather.2.cloned.1.call-done), kind=kLoop, calls=%fused_computation.2 | loop fusion | flops 12484480 | bytes 8323584 | tf_op jit(solution)/shard_map/reduce_sum | solution.py:110
  131.0 1.5 fusion.67
  132.5 10.1 %all_to_all.23 = f32[8,1,32]{2,1,0:T(1,128)S(1)} all-to-all(f32[8,1,32]{2,1,0:T(1,128)S(1)} %broadcast_in_dim.20), channel_id=1, replica_groups=mesh['img_0'=4,'img_1'=8,'ori'=8] {'ori'}, dimensions={0} | all-to-all | bytes 2048 | tf_op jit(solution)/shard_map/all_to_all | solution.py:16
  142.8 7.7 %all_to_all.24 = f32[8,1,32]{2,1,0:T(1,128)S(1)} all-to-all(f32[8,1,32]{2,1,0:T(1,128)S(1)} %broadcast_in_dim.22), channel_id=1, replica_groups=mesh['img_0'=4,'img_1'=8,'ori'=8] {'ori'}, dimensions={0} | all-to-all | bytes 2048 | tf_op jit(solution)/shard_map/all_to_all | solution.py:16
  150.6 5.5 %fusion = bf16[16256,2,128]{0,2,1:T(8,128)(2,1)} fusion(bf16[32,1,16256]{2,0,1:T(8,128)(2,1)S(1)} %get-tuple-element.21, bf16[32,1,16256]{2,0,1:T(8,128)(2,1)S(1)} %get-tuple-element.20, f32[32,128]{1,0:T(8,128)S(1)} %get-tuple-element.19), kind=kOutput, calls=%fused_computation.1 | convolution fusion | flops 274665472 | bytes 10420224 | tf_op jit(solution)/shard_map/ick,io->kco/dot_general | solution.py:123
  156.1 20.1 %reshape.344 = bf16[32,508,2,128]{1,0,3,2:T(8,128)(2,1)} reshape(bf16[16256,2,128]{0,2,1:T(8,128)(2,1)} %fusion) | data formatting | bytes 16646144 | tf_op jit(solution)/shard_map/reshape | solution.py:30
  176.2 9.1 %slice_bitcast_fusion = bf16[4,8,260,2,128]{2,1,0,4,3:T(8,128)(2,1)} fusion(bf16[32,508,2,128]{1,0,3,2:T(8,128)(2,1)} %reshape.344), kind=kLoop, calls=%fused_computation.5 | loop fusion | bytes 8519680 | tf_op jit(solution)/shard_map/reshape | solution.py:40
  185.2 8.4 %copy.56 = bf16[4,8,260,2,128]{4,2,3,0,1:T(8,128)(2,1)} copy(bf16[4,8,260,2,128]{2,1,0,4,3:T(8,128)(2,1)} %slice_bitcast_fusion) | data formatting | bytes 8519680 | tf_op jit(solution)/shard_map/reshape | solution.py:40
  193.7 4.6 %split.8 = bf16[32,248,2,128]{1,0,3,2:T(8,128)(2,1)} slice(bf16[32,508,2,128]{1,0,3,2:T(8,128)(2,1)} %reshape.344), slice={[0:32], [0:248], [0:2], [0:128]} | slice | bytes 8126464 | tf_op jit(solution)/shard_map/split | solution.py:52
  198.3 7.9 %copy.65 = bf16[32,248,2,128]{3,1,2,0:T(8,128)(2,1)} copy(bf16[32,248,2,128]{1,0,3,2:T(8,128)(2,1)} %split.8) | data formatting | bytes 8126464
  206.3 39.3 %reduce-scatter.9.cloned.1.call-done = bf16[4,260,2,128]{3,1,2,0:T(8,128)(2,1)} async-done(((bf16[32,260,2,128]{3,1,2,0:T(8,128)(2,1)}), bf16[4,260,2,128]{3,1,2,0:T(8,128)(2,1)}) %reduce-scatter.9.cloned.1.call-update) | async-done | bytes 532496 | tf_op jit(solution)/shard_map/reduce_scatter | solution.py:43
  245.7 49.5 %reduce-scatter.5.cloned.1.call-done = bf16[8,248,2,128]{3,1,2,0:T(8,128)(2,1)} async-done(((bf16[32,248,2,128]{3,1,2,0:T(8,128)(2,1)}), bf16[8,248,2,128]{3,1,2,0:T(8,128)(2,1)}) %reduce-scatter.5.cloned.1.call-update) | async-done | bytes 1015824 | tf_op jit(solution)/shard_map/reduce_scatter | solution.py:43
  295.2 0.6 broadcast_in_dim.23
  295.8 8.0 %all-to-all-start.2 = ((f32[32,1,128]{2,1,0:T(1,128)}), f32[32,1,128]{2,1,0:T(1,128)S(1)}, u32[]{:S(2)}, u32[]{:S(2)}) async-start(f32[32,1,128]{2,1,0:T(1,128)} %broadcast_in_dim.23), calls=%async_computation.6 | async-start | bytes 32768 | tf_op jit(solution)/shard_map/all_to_all | solution.py:16
  303.8 1.1 constant_dynamic-slice_fusion
  305.0 7.5 %all-to-all-done.2 = f32[32,1,128]{2,1,0:T(1,128)S(1)} async-done(((f32[32,1,128]{2,1,0:T(1,128)}), f32[32,1,128]{2,1,0:T(1,128)S(1)}, u32[]{:S(2)}, u32[]{:S(2)}) %all-to-all-start.2) | async-done | bytes 16416 | tf_op jit(solution)/shard_map/all_to_all | solution.py:16
  312.5 6.9 %reduce-scatter.11.cloned.1.call-done = bf16[1,260,2,128]{3,1,2,0:T(8,128)(2,1)} async-done(((bf16[4,260,2,128]{3,1,2,0:T(8,128)(2,1)}), bf16[1,260,2,128]{3,1,2,0:T(8,128)(2,1)}) %reduce-scatter.11.cloned.1.call-update) | async-done | bytes 133136 | tf_op jit(solution)/shard_map/reduce_scatter | solution.py:43
  319.4 38.5 %reduce-scatter.7.cloned.1.call-done = bf16[1,248,2,128]{3,1,2,0:T(8,128)(2,1)} async-done(((bf16[8,248,2,128]{3,1,2,0:T(8,128)(2,1)}), bf16[1,248,2,128]{3,1,2,0:T(8,128)(2,1)}) %reduce-scatter.7.cloned.1.call-update) | async-done | bytes 126992 | tf_op jit(solution)/shard_map/reduce_scatter | solution.py:43
  357.8 1.0 bitcast_subtract_fusion
  358.9 1.2 fusion.39
  360.1 0.4 fusion.12
  360.5 1.1 broadcast_in_dim.24
  361.6 9.9 %all-to-all-start.3 = ((bf16[8,64,2,508]{3,1,2,0:T(8,128)(2,1)}), bf16[8,64,2,508]{3,1,2,0:T(8,128)(2,1)S(1)}, u32[]{:S(2)}, u32[]{:S(2)}) async-start(bf16[8,64,2,508]{3,1,2,0:T(8,128)(2,1)} %broadcast_in_dim.24), calls=%async_computation.7 | async-start | bytes 2097152 | tf_op jit(solution)/shard_map/all_to_all | solution.py:16
  371.6 1.2 copy.59
  372.8 13.7 %all-to-all-done.3 = bf16[8,64,2,508]{3,1,2,0:T(8,128)(2,1)S(1)} async-done(((bf16[8,64,2,508]{3,1,2,0:T(8,128)(2,1)}), bf16[8,64,2,508]{3,1,2,0:T(8,128)(2,1)S(1)}, u32[]{:S(2)}, u32[]{:S(2)}) %all-to-all-start.3) | async-done | bytes 1040416 | tf_op jit(solution)/shard_map/all_to_all | solution.py:16
  386.6 0.9 copy.60
  (48 shorter events, 1.5 us)
Async XLA Ops:
  7.2 1.5 copy-start
  7.2 4.6 %copy-start.6 = (s32[1,512]{1,0:T(1,128)S(1)}, s32[1,512]{1,0:T(1,128)}, u32[]{:S(2)}) copy-start(s32[1,512]{1,0:T(1,128)} %param.10) | copy-start | bytes 6148
  7.2 4.7 %copy-start.8 = (s32[32]{0:T(128)S(1)}, s32[32]{0:T(128)}, u32[]{:S(2)}) copy-start(s32[32]{0:T(128)} %param.8) | copy-start | bytes 388
  7.2 4.7 %copy-start.2 = (bf16[32,2,16256]{2,1,0:T(2,128)(2,1)S(1)}, bf16[32,2,16256]{2,1,0:T(2,128)(2,1)}, u32[]{:S(2)}) copy-start(bf16[32,2,16256]{2,1,0:T(2,128)(2,1)} %param.7) | copy-start | bytes 6242308
  7.2 105.3 %all-gather.2.cloned.1.call-start = ((), (), s32[]{:S(2)}) async-start(), calls=%async_computation.8 | async-start | bytes 8583168 | tf_op jit(solution)/shard_map/all_gather | solution.py:103
  11.7 233.9 %reduce-scatter.9.cloned.1.call-start = ((), (), s32[]{:S(2)}) async-start(), calls=%async_computation.11 | async-start | bytes 4866048 | tf_op jit(solution)/shard_map/reduce_scatter | solution.py:43
  22.9 108.1 %copy-start.9 = (f32[32]{0:T(128)S(1)}, f32[32]{0:T(128)}, u32[]{:S(2)}) copy-start(f32[32]{0:T(128)} %param.9) | copy-start | bytes 388
  112.5 18.5 %copy-start.1 = (bf16[128,2,16256]{0,1,2:T(2,128)(2,1)S(1)}, bf16[128,2,16256]{0,1,2:T(2,128)(2,1)}, u32[]{:S(2)}) copy-start(bf16[128,2,16256]{0,1,2:T(2,128)(2,1)} %all-gather.2.cloned.1.call-done) | copy-start | bytes 24969220
  150.5 5.6 %copy-start.5 = (f32[32,128]{1,0:T(8,128)}, f32[32,128]{1,0:T(8,128)S(1)}, u32[]{:S(2)}) copy-start(f32[32,128]{1,0:T(8,128)S(1)} %get-tuple-element.19) | copy-start | bytes 49156
  193.6 101.5 %reduce-scatter.5.cloned.1.call-start = ((), (), s32[]{:S(2)}) async-start(), calls=%async_computation.9 | async-start | bytes 5079040 | tf_op jit(solution)/shard_map/reduce_scatter | solution.py:43
  206.2 152.7 %copy-start.7 = (f32[128]{0:T(128)S(1)}, f32[128]{0:T(128)}, u32[]{:S(2)}) copy-start(f32[128]{0:T(128)} %param.13) | copy-start | bytes 1540
  206.2 113.1 %reduce-scatter.11.cloned.1.call-start = ((), (), s32[]{:S(2)}) async-start(), calls=%async_computation.12 | async-start | bytes 675840 | tf_op jit(solution)/shard_map/reduce_scatter | solution.py:43
  245.6 112.2 %reduce-scatter.7.cloned.1.call-start = ((), (), s32[]{:S(2)}) async-start(), calls=%async_computation.10 | async-start | bytes 1142784 | tf_op jit(solution)/shard_map/reduce_scatter | solution.py:43
  295.8 16.6 %all-to-all-start.2 = ((f32[32,1,128]{2,1,0:T(1,128)}), f32[32,1,128]{2,1,0:T(1,128)S(1)}, u32[]{:S(2)}, u32[]{:S(2)}) async-start(f32[32,1,128]{2,1,0:T(1,128)} %broadcast_in_dim.23), calls=%async_computation.6 | async-start | bytes 32768 | tf_op jit(solution)/shard_map/all_to_all | solution.py:16
  360.1 11.4 %copy-start.3 = (bf16[1,260,2,128]{3,1,2,0:T(8,128)(2,1)S(1)}, bf16[1,260,2,128]{3,1,2,0:T(8,128)(2,1)}, u32[]{:S(2)}) copy-start(bf16[1,260,2,128]{3,1,2,0:T(8,128)(2,1)} %reduce-scatter.11.cloned.1.call-done) | copy-start | bytes 399364
  360.1 11.4 %copy-start.4 = (bf16[1,248,2,128]{3,1,2,0:T(8,128)(2,1)S(1)}, bf16[1,248,2,128]{3,1,2,0:T(8,128)(2,1)}, u32[]{:S(2)}) copy-start(bf16[1,248,2,128]{3,1,2,0:T(8,128)(2,1)} %reduce-scatter.7.cloned.1.call-done) | copy-start | bytes 380932
  361.6 24.8 %all-to-all-start.3 = ((bf16[8,64,2,508]{3,1,2,0:T(8,128)(2,1)}), bf16[8,64,2,508]{3,1,2,0:T(8,128)(2,1)S(1)}, u32[]{:S(2)}, u32[]{:S(2)}) async-start(bf16[8,64,2,508]{3,1,2,0:T(8,128)(2,1)} %broadcast_in_dim.24), calls=%async_computation.7 | async-start | bytes 2097152 | tf_op jit(solution)/shard_map/all_to_all | solution.py:16
Sparse Core Ops, SparseCore 0:
  11.8 100.6 all-gather.1
  193.8 51.7 reduce-scatter.8
  248.2 46.9 reduce-scatter.4
  297.6 21.7 reduce-scatter.10
  321.7 36.0 reduce-scatter.6
where the time goes:
time: 395 us; the launch traced here: 394 us
  waiting for transfers between devices  245 us (62%)
  local copies, waits for them, and re-layouts  60.2 us (15%)
  other arithmetic  31.3 us (8%)
  starting transfers between devices  18.1 us (5%)
  blocking collectives  17.7 us (4%)
  between operations  14.1 us (4%)
  matrix products  7.7 us (2%)
    reduce_scatter x4, waiting for transfers between devices, own_block(): tiles = lax.psum_scatter(tiles, axes[k], scatter_dimension=0, tiled=True)  134 us
    all_gather x1, waiting for transfers between devices, shards(): slices = lax.all_gather(own_part, IMG, axis=2, tiled=True)  89.6 us
    all_to_all x2, waiting for transfers between devices, sent_to_all(): lax.all_to_all(jnp.broadcast_to(x[None], (devices, *x.shape)), axis, 0, 0...  21.2 us
    reshape x1, local copies, waits for them, and re-layouts, split_up(): return jnp.moveaxis(x.reshape(*before, devices, -1, *after), dim, 0)  20.1 us
    reduce_sum x1, other arithmetic, shards(): energies = jnp.sum(jnp.square(slices.astype(jnp.float32)), axis=(1, 2))  18.5 us
    all_to_all x2, starting transfers between devices, sent_to_all(): lax.all_to_all(jnp.broadcast_to(x[None], (devices, *x.shape)), axis, 0, 0...  17.9 us
    all_to_all x2, blocking collectives, sent_to_all(): lax.all_to_all(jnp.broadcast_to(x[None], (devices, *x.shape)), axis, 0, 0...  17.7 us
    reshape x2, local copies, waits for them, and re-layouts, own_block(): tiles = tiles.reshape(*(lax.axis_size(a) for a in axes), *inside)  17.5 us
  transfers between devices with their start and end apart: 7, of which 7 were waited for; matrix products, arithmetic and copies ran while one was open for 7% of the time, Pallas kernels for 0%

commit v1 on v0

--- a/solution.py
+++ b/solution.py
@@ -100,7 +100,9 @@
     column_start = lax.axis_index(IMG) * part_width
     orient_ids = lax.axis_index("ori") * local_orients + jnp.arange(local_orients, dtype=jnp.int32)
     own_part = project_piece(volume, column_start, tilts, azimuth)
-    slices = lax.all_gather(own_part, IMG, axis=2, tiled=True)
+    slices = jnp.concatenate(
+        lax.all_to_all(jnp.stack([own_part] * lax.axis_size(IMG)), IMG, 0, 0), axis=2
+    )
     rotated = rotate_images(images, shifts)
     flat_images = rotated.reshape(image_count, 2 * full_width)
     flat_slices = slices.reshape(local_orients, 2 * full_width)

time: 395 us -> 543 us (1.37)
  waiting for transfers between devices: 245 us -> 339 us
  local copies, waits for them, and re-layouts: 60.2 us -> 96.5 us
  starting transfers between devices: 18.1 us -> 29.9 us
    all_to_all x0 -> x1, waiting for transfers between devices: none -> 173 us  [shards(): lax.all_to_all(jnp.stack([own_part] * lax.axis_size(IMG)), IMG, 0, 0)]
    all_gather x1 -> x0, waiting for transfers between devices: 89.6 us -> none  [shards(): slices = lax.all_gather(own_part, IMG, axis=2, tiled=True)]
    another operation x0 -> x2, local copies, waits for them, and re-layouts: none -> 20.2 us  [the longest x1 14.6 us: shards(): flat_slices = slices.reshape(local_orients, 2 * full_width)]
    reshape x0 -> x1, local copies, waits for them, and re-layouts: none -> 15.4 us  [shards(): jnp.concatenate(lax.all_to_all(jnp.stack([own_part] * lax.axis_size(IMG))...]
    all_to_all x0 -> x1, starting transfers between devices: none -> 12.3 us  [shards(): lax.all_to_all(jnp.stack([own_part] * lax.axis_size(IMG)), IMG, 0, 0)]
    reduce_scatter x4, waiting for transfers between devices: 134 us -> 144 us  [own_block(): tiles = lax.psum_scatter(tiles, axes[k], scatter_dimension=0, tiled=True)]
  transfers between devices with their start and end apart: 7 -> 7, of which waited for: 7 -> 7; matrix products, arithmetic and copies ran while one was open for 7% -> 5% of each run, Pallas kernels for 0% -> 0%
where the time goes in v1:
time: 543 us; the launch traced here: 541 us
  waiting for transfers between devices  339 us (62%)
  local copies, waits for them, and re-layouts  96.5 us (18%)
  other arithmetic  31.4 us (6%)
  starting transfers between devices  29.9 us (6%)
  blocking collectives  18 us (3%)
  between operations  14 us (3%)
  matrix products  13.1 us (2%)
    all_to_all x1, waiting for transfers between devices, shards(): lax.all_to_all(jnp.stack([own_part] * lax.axis_size(IMG)), IMG, 0, 0)  173 us
    reduce_scatter x4, waiting for transfers between devices, own_block(): tiles = lax.psum_scatter(tiles, axes[k], scatter_dimension=0, tiled=True)  144 us
    all_to_all x2, waiting for transfers between devices, sent_to_all(): lax.all_to_all(jnp.broadcast_to(x[None], (devices, *x.shape)), axis, 0, 0...  21.2 us
    reshape x1, local copies, waits for them, and re-layouts, split_up(): return jnp.moveaxis(x.reshape(*before, devices, -1, *after), dim, 0)  20.1 us
    reduce_sum x1, other arithmetic, shards(): energies = jnp.sum(jnp.square(slices.astype(jnp.float32)), axis=(1, 2))  18.4 us
    all_to_all x2, blocking collectives, sent_to_all(): lax.all_to_all(jnp.broadcast_to(x[None], (devices, *x.shape)), axis, 0, 0...  18 us
    reshape x2, local copies, waits for them, and re-layouts, own_block(): tiles = tiles.reshape(*(lax.axis_size(a) for a in axes), *inside)  17.5 us
    all_to_all x2, starting transfers between devices, sent_to_all(): lax.all_to_all(jnp.broadcast_to(x[None], (devices, *x.shape)), axis, 0, 0...  17.5 us
  transfers between devices with their start and end apart: 7, of which 7 were waited for; matrix products, arithmetic and copies ran while one was open for 5% of the time, Pallas kernels for 0%

profile of v1, /device:TPU:1, one launch (start us, length us, event | category | flops | bytes accessed | tf_op | source)
XLA Modules:
  0.0 541.5 jit_solution(14305668239994969168)
XLA Ops:
  7.2 1.1 reshape.357
  8.7 1.8 fusion.29
  10.7 5.6 %stack.11 = bf16[32,128,2,508]{1,2,3,0:T(2,128)(2,1)} broadcast(bf16[128,2,508]{0,1,2:T(2,128)(2,1)S(1)} %copy.58), dimensions={1,2,3} | broadcast | bytes 8583168 | tf_op jit(solution)/shard_map/stack | solution.py:104
  16.3 12.3 %all-to-all-start = ((bf16[32,128,2,508]{1,2,3,0:T(2,128)(2,1)}), bf16[32,128,2,508]{1,2,3,0:T(2,128)(2,1)}, u32[]{:S(2)}, u32[]{:S(2)}) async-start(bf16[32,128,2,508]{1,2,3,0:T(2,128)(2,1)} %stack.11), calls=%async_computation | async-start | bytes 16646144 | tf_op jit(solution)/shard_map/all_to_all | solution.py:104
  28.7 3.0 fusion.52
  31.7 8.0 %fusion.6 = (bf16[32,1,16256]{2,0,1:T(8,128)(2,1)S(1)}, bf16[32,1,16256]{2,0,1:T(8,128)(2,1)S(1)}) fusion(f32[16256]{0:T(1024)S(1)} %fusion.35, f32[32]{0:T(128)S(1)} %convert_multiply_fusion, bf16[32,1,16256]{2,1,0:T(2,128)(2,1)S(1)} %get-tuple-element.23, bf16[32,1,16256]{2,1,0:T(2,128)(2,1)S(1)} %get-tuple-element.22), kind=kLoop, calls=%fused_computation.12 | loop fusion | flops 5722112 | bytes 4226688 | tf_op jit(solution)/shard_map/convert.2
  39.9 1.5 copy.80
  41.6 173.4 %all-to-all-done = bf16[32,128,2,508]{1,2,3,0:T(2,128)(2,1)} async-done(((bf16[32,128,2,508]{1,2,3,0:T(2,128)(2,1)}), bf16[32,128,2,508]{1,2,3,0:T(2,128)(2,1)}, u32[]{:S(2)}, u32[]{:S(2)}) %all-to-all-start) | async-done | bytes 8323104 | tf_op jit(solution)/shard_map/all_to_all | solution.py:104
  214.9 18.4 %multiply_reduce_fusion = f32[128]{0:T(128)S(1)} fusion(bf16[32,128,2,508]{1,2,3,0:T(2,128)(2,1)} %all-to-all-done), kind=kLoop, calls=%fused_computation.2 | loop fusion | flops 12484480 | bytes 8323584 | tf_op jit(solution)/shard_map/reduce_sum | solution.py:112
  233.3 15.4 %copy.59 = bf16[128,2,32,508]{3,2,1,0:T(8,128)(2,1)} copy(bf16[128,2,32,508]{0,1,3,2:T(2,128)(2,1)} %bitcast.3) | data formatting | bytes 16646144 | tf_op jit(solution)/shard_map/reshape | solution.py:103
  248.7 14.6 %reshape_reshape.3 = bf16[128,32512]{1,0:T(8,128)(2,1)} reshape(bf16[128,2,32,508]{3,2,1,0:T(8,128)(2,1)} %copy.59) | data formatting | bytes 16646144 | tf_op jit(solution)/shard_map/reshape;reshape | solution.py:108
  263.4 6.9 %fusion.53 = (f32[32]{0:T(128)S(1)}, f32[32,128]{1,0:T(8,128)S(1)}) fusion(f32[128]{0:T(128)S(1)} %broadcast_multiply_fusion, bf16[32,32512]{1,0:T(8,128)(2,1)} %bitcast.43, bf16[128,32512]{1,0:T(8,128)(2,1)} %reshape_reshape.3, f32[32]{0:T(128)S(1)} %copy-done.7, pred[128]{0:T(512)(128)(4,1)S(1)} %compare_reduce_fusion), kind=kOutput, calls=%fused_computation.79 | convolution fusion | flops 266358752 | bytes 10421120 | tf_op jit(solution)/shard_map/dot_general | solution.py:109
  270.3 10.2 %all_to_all.28 = f32[8,1,32]{2,1,0:T(1,128)S(1)} all-to-all(f32[8,1,32]{2,1,0:T(1,128)S(1)} %broadcast_in_dim.20), channel_id=1, replica_groups=mesh['img_0'=4,'img_1'=8,'ori'=8] {'ori'}, dimensions={0} | all-to-all | bytes 2048 | tf_op jit(solution)/shard_map/all_to_all | solution.py:16
  280.7 7.8 %all_to_all.29 = f32[8,1,32]{2,1,0:T(1,128)S(1)} all-to-all(f32[8,1,32]{2,1,0:T(1,128)S(1)} %broadcast_in_dim.22), channel_id=1, replica_groups=mesh['img_0'=4,'img_1'=8,'ori'=8] {'ori'}, dimensions={0} | all-to-all | bytes 2048 | tf_op jit(solution)/shard_map/all_to_all | solution.py:16
  288.6 5.5 %fusion = bf16[16256,2,128]{0,2,1:T(8,128)(2,1)} fusion(bf16[32,1,16256]{2,0,1:T(8,128)(2,1)S(1)} %get-tuple-element.21, bf16[32,1,16256]{2,0,1:T(8,128)(2,1)S(1)} %get-tuple-element.20, f32[32,128]{1,0:T(8,128)S(1)} %get-tuple-element.19), kind=kOutput, calls=%fused_computation.1 | convolution fusion | flops 274665472 | bytes 10420224 | tf_op jit(solution)/shard_map/ick,io->kco/dot_general | solution.py:125
  294.2 20.1 %reshape.365 = bf16[32,508,2,128]{1,0,3,2:T(8,128)(2,1)} reshape(bf16[16256,2,128]{0,2,1:T(8,128)(2,1)} %fusion) | data formatting | bytes 16646144 | tf_op jit(solution)/shard_map/reshape | solution.py:30
  314.3 9.1 %slice_bitcast_fusion = bf16[4,8,260,2,128]{2,1,0,4,3:T(8,128)(2,1)} fusion(bf16[32,508,2,128]{1,0,3,2:T(8,128)(2,1)} %reshape.365), kind=kLoop, calls=%fused_computation.3 | loop fusion | bytes 8519680 | tf_op jit(solution)/shard_map/reshape | solution.py:40
  323.3 8.4 %copy.64 = bf16[4,8,260,2,128]{4,2,3,0,1:T(8,128)(2,1)} copy(bf16[4,8,260,2,128]{2,1,0,4,3:T(8,128)(2,1)} %slice_bitcast_fusion) | data formatting | bytes 8519680 | tf_op jit(solution)/shard_map/reshape | solution.py:40
  331.8 4.6 split.8
  336.4 7.9 %copy.76 = bf16[32,248,2,128]{3,1,2,0:T(8,128)(2,1)} copy(bf16[32,248,2,128]{1,0,3,2:T(8,128)(2,1)} %split.8) | data formatting | bytes 8126464
  344.4 48.5 %reduce-scatter.9.cloned.1.call-done = bf16[4,260,2,128]{3,1,2,0:T(8,128)(2,1)} async-done(((bf16[32,260,2,128]{3,1,2,0:T(8,128)(2,1)}), bf16[4,260,2,128]{3,1,2,0:T(8,128)(2,1)}) %reduce-scatter.9.cloned.1.call-update) | async-done | bytes 532496 | tf_op jit(solution)/shard_map/reduce_scatter | solution.py:43
  392.9 49.5 %reduce-scatter.5.cloned.1.call-done = bf16[8,248,2,128]{3,1,2,0:T(8,128)(2,1)} async-done(((bf16[32,248,2,128]{3,1,2,0:T(8,128)(2,1)}), bf16[8,248,2,128]{3,1,2,0:T(8,128)(2,1)}) %reduce-scatter.5.cloned.1.call-update) | async-done | bytes 1015824 | tf_op jit(solution)/shard_map/reduce_scatter | solution.py:43
  443.0 8.0 %all-to-all-start.3 = ((f32[32,1,128]{2,1,0:T(1,128)}), f32[32,1,128]{2,1,0:T(1,128)S(1)}, u32[]{:S(2)}, u32[]{:S(2)}) async-start(f32[32,1,128]{2,1,0:T(1,128)} %broadcast_in_dim.23), calls=%async_computation.7 | async-start | bytes 32768 | tf_op jit(solution)/shard_map/all_to_all | solution.py:16
  451.0 1.1 constant_dynamic-slice_fusion
  452.2 7.5 %all-to-all-done.3 = f32[32,1,128]{2,1,0:T(1,128)S(1)} async-done(((f32[32,1,128]{2,1,0:T(1,128)}), f32[32,1,128]{2,1,0:T(1,128)S(1)}, u32[]{:S(2)}, u32[]{:S(2)}) %all-to-all-start.3) | async-done | bytes 16416 | tf_op jit(solution)/shard_map/all_to_all | solution.py:16
  459.7 7.1 %reduce-scatter.11.cloned.1.call-done = bf16[1,260,2,128]{3,1,2,0:T(8,128)(2,1)} async-done(((bf16[4,260,2,128]{3,1,2,0:T(8,128)(2,1)}), bf16[1,260,2,128]{3,1,2,0:T(8,128)(2,1)}) %reduce-scatter.11.cloned.1.call-update) | async-done | bytes 133136 | tf_op jit(solution)/shard_map/reduce_scatter | solution.py:43
  466.7 39.0 %reduce-scatter.7.cloned.1.call-done = bf16[1,248,2,128]{3,1,2,0:T(8,128)(2,1)} async-done(((bf16[8,248,2,128]{3,1,2,0:T(8,128)(2,1)}), bf16[1,248,2,128]{3,1,2,0:T(8,128)(2,1)}) %reduce-scatter.7.cloned.1.call-update) | async-done | bytes 126992 | tf_op jit(solution)/shard_map/reduce_scatter | solution.py:43
  506.7 1.2 fusion.26
  508.4 1.1 broadcast_in_dim.24
  509.5 9.4 %all-to-all-start.4 = ((bf16[8,64,2,508]{3,1,2,0:T(8,128)(2,1)}), bf16[8,64,2,508]{3,1,2,0:T(8,128)(2,1)S(1)}, u32[]{:S(2)}, u32[]{:S(2)}) async-start(bf16[8,64,2,508]{3,1,2,0:T(8,128)(2,1)} %broadcast_in_dim.24), calls=%async_computation.8 | async-start | bytes 2097152 | tf_op jit(solution)/shard_map/all_to_all | solution.py:16
  519.0 1.2 copy.68
  520.2 13.7 %all-to-all-done.4 = bf16[8,64,2,508]{3,1,2,0:T(8,128)(2,1)S(1)} async-done(((bf16[8,64,2,508]{3,1,2,0:T(8,128)(2,1)}), bf16[8,64,2,508]{3,1,2,0:T(8,128)(2,1)S(1)}, u32[]{:S(2)}, u32[]{:S(2)}) %all-to-all-start.4) | async-done | bytes 1040416 | tf_op jit(solution)/shard_map/all_to_all | solution.py:16
  (50 shorter events, 4.8 us)
Async XLA Ops:
  7.2 1.3 copy-start
  16.3 12.3 %copy-start.8 = (s32[32]{0:T(128)S(1)}, s32[32]{0:T(128)}, u32[]{:S(2)}) copy-start(s32[32]{0:T(128)} %param.8) | copy-start | bytes 388
  16.3 12.4 %copy-start.1 = (bf16[32,2,16256]{2,1,0:T(2,128)(2,1)S(1)}, bf16[32,2,16256]{2,1,0:T(2,128)(2,1)}, u32[]{:S(2)}) copy-start(bf16[32,2,16256]{2,1,0:T(2,128)(2,1)} %param.7) | copy-start | bytes 6242308
  16.3 198.6 %all-to-all-start = ((bf16[32,128,2,508]{1,2,3,0:T(2,128)(2,1)}), bf16[32,128,2,508]{1,2,3,0:T(2,128)(2,1)}, u32[]{:S(2)}, u32[]{:S(2)}) async-start(bf16[32,128,2,508]{1,2,3,0:T(2,128)(2,1)} %stack.11), calls=%async_computation | async-start | bytes 16646144 | tf_op jit(solution)/shard_map/all_to_all | solution.py:104
  28.6 364.2 %reduce-scatter.9.cloned.1.call-start = ((), (), s32[]{:S(2)}) async-start(), calls=%async_computation.11 | async-start | bytes 4866048 | tf_op jit(solution)/shard_map/reduce_scatter | solution.py:43
  39.9 1.5 copy-start.5
  248.7 14.6 %copy-start.7 = (f32[32]{0:T(128)S(1)}, f32[32]{0:T(128)}, u32[]{:S(2)}) copy-start(f32[32]{0:T(128)} %param.9) | copy-start | bytes 388
  288.6 5.6 %copy-start.4 = (f32[32,128]{1,0:T(8,128)}, f32[32,128]{1,0:T(8,128)S(1)}, u32[]{:S(2)}) copy-start(f32[32,128]{1,0:T(8,128)S(1)} %get-tuple-element.19) | copy-start | bytes 49156
  331.7 110.6 %reduce-scatter.5.cloned.1.call-start = ((), (), s32[]{:S(2)}) async-start(), calls=%async_computation.9 | async-start | bytes 5079040 | tf_op jit(solution)/shard_map/reduce_scatter | solution.py:43
  344.3 162.4 %copy-start.6 = (f32[128]{0:T(128)S(1)}, f32[128]{0:T(128)}, u32[]{:S(2)}) copy-start(f32[128]{0:T(128)} %param.13) | copy-start | bytes 1540
  344.3 122.4 %reduce-scatter.11.cloned.1.call-start = ((), (), s32[]{:S(2)}) async-start(), calls=%async_computation.12 | async-start | bytes 675840 | tf_op jit(solution)/shard_map/reduce_scatter | solution.py:43
  392.8 112.9 %reduce-scatter.7.cloned.1.call-start = ((), (), s32[]{:S(2)}) async-start(), calls=%async_computation.10 | async-start | bytes 1142784 | tf_op jit(solution)/shard_map/reduce_scatter | solution.py:43
  443.0 16.6 %all-to-all-start.3 = ((f32[32,1,128]{2,1,0:T(1,128)}), f32[32,1,128]{2,1,0:T(1,128)S(1)}, u32[]{:S(2)}, u32[]{:S(2)}) async-start(f32[32,1,128]{2,1,0:T(1,128)} %broadcast_in_dim.23), calls=%async_computation.7 | async-start | bytes 32768 | tf_op jit(solution)/shard_map/all_to_all | solution.py:16
  507.9 11.0 %copy-start.2 = (bf16[1,260,2,128]{3,1,2,0:T(8,128)(2,1)S(1)}, bf16[1,260,2,128]{3,1,2,0:T(8,128)(2,1)}, u32[]{:S(2)}) copy-start(bf16[1,260,2,128]{3,1,2,0:T(8,128)(2,1)} %reduce-scatter.11.cloned.1.call-done) | copy-start | bytes 399364
  507.9 11.0 %copy-start.3 = (bf16[1,248,2,128]{3,1,2,0:T(8,128)(2,1)S(1)}, bf16[1,248,2,128]{3,1,2,0:T(8,128)(2,1)}, u32[]{:S(2)}) copy-start(bf16[1,248,2,128]{3,1,2,0:T(8,128)(2,1)} %reduce-scatter.7.cloned.1.call-done) | copy-start | bytes 380932
  509.5 24.4 %all-to-all-start.4 = ((bf16[8,64,2,508]{3,1,2,0:T(8,128)(2,1)}), bf16[8,64,2,508]{3,1,2,0:T(8,128)(2,1)S(1)}, u32[]{:S(2)}, u32[]{:S(2)}) async-start(bf16[8,64,2,508]{3,1,2,0:T(8,128)(2,1)} %broadcast_in_dim.24), calls=%async_computation.8 | async-start | bytes 2097152 | tf_op jit(solution)/shard_map/all_to_all | solution.py:16
Sparse Core Ops, SparseCore 0:
  331.9 60.9 reduce-scatter.8
  395.4 46.9 reduce-scatter.4
  444.9 21.7 reduce-scatter.10
  469.1 36.5 reduce-scatter.6
